TPU v7x, 256 devices: a whole 4x4x8 slice. The times are simulated.
256 devices in a mesh: view: 16 (over z, y_hi), tok: 16 (over y_lo, x, core).
Axes of the slice: x: 4, y: 4 (y_hi: 2, y_lo: 2; y = y_hi * 2 + y_lo), z: 8, core: 2. Of those that a mesh axis runs over, the one named last changes fastest.
Arguments:
- q1: bfloat16 [16, 512, 1024], P('view', 'tok'), may hold values from -96 to 96
- k1: bfloat16 [16, 512, 1024], P('view', 'tok'), may hold values from -6 to 6
- v1: bfloat16 [16, 512, 1024], P('view', 'tok'), may hold values from -6 to 6
- nbr: int32 [16, 7], P('view'), may hold values from 0 to 15, as said below
- x2: bfloat16 [16, 512, 1024], P('view', 'tok'), may hold values from -6 to 6
- w_view_out: bfloat16 [1024, 1024], replicated, may hold values from -0.1875 to 0.1875
- norm_gain: float32 [1024], replicated, may hold values from 0.5 to 1.5
- w_qkv: bfloat16 [1024, 3072], replicated, may hold values from -0.1875 to 0.1875
- w_out: bfloat16 [1024, 1024], replicated, may hold values from -0.1875 to 0.1875
Outputs:
- view_feats: float32 [16, 512, 1024], P('view', 'tok')
- lrm_out: float32 [16, 512, 1024], P('view', 'tok')
Inputs may be any that keep to these rules, and one draw needn't show every extreme that they name: `nbr`: row v lists 7 distinct view indices, none equal to v.
All inputs are finite; a program needn't handle non-finite values.
Results may differ from a plain program's by a relative error of at most 0.014.
Values may be sent and summed in bfloat16 or wider, within the bound.
A program may use at most 128 MiB of HBM per device.

v0:
```python
import jax
import jax.numpy as jnp
from jax import lax
from jax.sharding import PartitionSpec as P

H1 = 16
HD1 = 64
HD2 = 64
EPSILON = 1e-06
NEGATIVE = -1e30


def absorb(running, queries, key_piece, val_piece, keep_key, factor_scale):
    running_max, row_total, weighted = running
    scores = (
        jnp.einsum("qhd,khd->qhk", queries, key_piece, preferred_element_type=jnp.float32)
        * factor_scale
    )
    scores = jnp.where(keep_key[None, None, :], scores, NEGATIVE)
    new_max = jnp.maximum(running_max, jnp.max(scores, axis=-1))
    weights = jnp.where(keep_key[None, None, :], jnp.exp(scores - new_max[..., None]), 0.0)
    row_total = jnp.sum(weights, axis=-1)
    weighted = jnp.einsum(
        "qhk,khd->qhd", weights.astype(jnp.bfloat16), val_piece, preferred_element_type=jnp.float32
    )
    return (new_max, row_total, weighted)


def per_device(q1, k1, v1, nbr, x2, w_view_out, norm_gain, w_qkv, w_out):
    own_view = lax.axis_index("view")
    wanted = nbr[0]
    queries = lax.all_gather(q1, "tok", axis=1, tiled=True)[0].reshape(-1, H1, HD1)
    query_rows = queries.shape[0]
    start_state = (
        jnp.full((query_rows, H1), NEGATIVE, jnp.float32),
        jnp.zeros((query_rows, H1), jnp.float32),
        jnp.zeros((query_rows, H1, HD1), jnp.float32),
    )
    scale_one = HD1 ** (-0.5)
    key_piece = lax.all_gather(k1, "view", axis=0, tiled=True)
    val_piece = lax.all_gather(v1, "view", axis=0, tiled=True)
    view_ids = jnp.arange(key_piece.shape[0], dtype=jnp.int32)
    keep_view = (view_ids == own_view) | jnp.any(view_ids[:, None] == wanted[None, :], axis=1)
    keep_key = jnp.repeat(keep_view, key_piece.shape[1])
    running_max, row_total, weighted = absorb(
        start_state,
        queries,
        key_piece.reshape(-1, H1, HD1),
        val_piece.reshape(-1, H1, HD1),
        keep_key,
        scale_one,
    )
    tok_devs = lax.axis_size("tok")
    my_rows = query_rows // tok_devs
    row_peak = lax.pmax(running_max, "tok")
    factor = jnp.exp(running_max - row_peak)
    summed, totals = (
        lax.psum_scatter(weighted * factor[..., None], "tok", scatter_dimension=0, tiled=True),
        lax.psum_scatter(row_total * factor, "tok", scatter_dimension=0, tiled=True),
    )
    attn_one = (summed / totals[..., None]).reshape(my_rows, -1)
    features = attn_one * lax.rsqrt(jnp.mean(attn_one * attn_one, axis=-1, keepdims=True) + EPSILON)
    features_half = features.astype(jnp.bfloat16)
    hidden = x2[0].astype(jnp.float32) + jnp.dot(
        features_half, w_view_out, preferred_element_type=jnp.float32
    )
    normed = (
        hidden * lax.rsqrt(jnp.mean(hidden * hidden, axis=-1, keepdims=True) + EPSILON) * norm_gain
    ).astype(jnp.bfloat16)
    projected = (
        jnp.dot(normed, w_qkv, preferred_element_type=jnp.float32)
        .astype(jnp.bfloat16)
        .reshape(my_rows, 3, -1)
    )
    by_head = lax.all_to_all(projected, "tok", split_axis=2, concat_axis=0, tiled=True)
    local_heads = by_head.shape[2] // HD2
    head_queries = by_head[:, 0].reshape(-1, local_heads, HD2)
    view_rows = head_queries.shape[0]
    scale_two = HD2 ** (-0.5)
    second_state = (
        jnp.full((view_rows, local_heads), NEGATIVE, jnp.float32),
        jnp.zeros((view_rows, local_heads), jnp.float32),
        jnp.zeros((view_rows, local_heads, HD2), jnp.float32),
    )
    key_piece = lax.all_gather(by_head[:, 1], "view", axis=0, tiled=True)
    val_piece = lax.all_gather(by_head[:, 2], "view", axis=0, tiled=True)
    keep_key = jnp.ones((key_piece.shape[0],), jnp.bool_)
    second_max, second_total, second_sum = absorb(
        second_state,
        head_queries,
        key_piece.reshape(-1, local_heads, HD2),
        val_piece.reshape(-1, local_heads, HD2),
        keep_key,
        scale_two,
    )
    attn_two = (second_sum / second_total[..., None]).reshape(view_rows, -1).astype(jnp.bfloat16)
    returned = lax.all_to_all(attn_two, "tok", split_axis=0, concat_axis=1, tiled=True)
    wide = returned.astype(jnp.float32)
    unit_rows = (wide * lax.rsqrt(jnp.mean(wide * wide, axis=-1, keepdims=True) + EPSILON)).astype(
        jnp.bfloat16
    )
    result = jnp.dot(unit_rows, w_out, preferred_element_type=jnp.float32)
    return (features[None], result[None])


def solution(mesh):
    return jax.shard_map(
        per_device,
        mesh=mesh,
        in_specs=(
            P("view", "tok", None),
            P("view", "tok", None),
            P("view", "tok", None),
            P("view", None),
            P("view", "tok", None),
            P(),
            P(),
            P(),
            P(),
        ),
        out_specs=(P("view", "tok", None), P("view", "tok", None)),
        check_vma=False,
    )
```

profile of v0, /device:TPU:1, one launch (start us, length us, event | category | flops | bytes accessed | tf_op | source)
XLA Modules:
  0.0 568.1 jit_solution(11776893962329701940)
XLA Ops:
  7.2 0.7 all-gather.8.cloned.1.call-update
  8.0 0.7 all-gather.10.cloned.1.call-update
  8.7 0.7 all-gather.12.cloned.1.call-update
  9.4 0.7 fusion.49
  10.3 0.1 broadcast_in_dim.58
  10.4 78.4 %all-gather.8.cloned.1.call-done = bf16[16,32,1024]{2,1,0:T(8,128)(2,1)} async-done(((bf16[1,32,1024]{2,1,0:T(8,128)(2,1)}), bf16[16,32,1024]{2,1,0:T(8,128)(2,1)}) %all-gather.8.cloned.1.call-update) | async-done | bytes 1048592 | tf_op jit(solution)/shard_map/all_gather | solution.py:40
  88.8 4.1 reshape.120
  92.8 33.8 %all-gather.10.cloned.1.call-done = bf16[1,512,1024]{2,1,0:T(8,128)(2,1)} async-done(((bf16[1,32,1024]{2,1,0:T(8,128)(2,1)}), bf16[1,512,1024]{2,1,0:T(8,128)(2,1)}) %all-gather.10.cloned.1.call-update) | async-done | bytes 1048592 | tf_op jit(solution)/shard_map/all_gather | solution.py:32
  126.6 1.5 copy.56
  128.1 9.1 %bitcast_reduce_fusion = (f32[512,16]{0,1:T(8,128)S(1)}, f32[16,512,512]{2,1,0:T(8,128)}) fusion(pred[512]{0:T(512)(128)(4,1)S(1)} %broadcast_in_dim.58, bf16[512,16,64]{0,2,1:T(8,128)(2,1)S(1)} %bitcast.104, bf16[512,16,64]{2,1,0:T(8,128)(2,1)} %reshape.120), kind=kOutput, calls=%fused_computation.3 | convolution fusion | flops 549445632 | bytes 18907648 | tf_op jit(solution)/shard_map/qhd,khd->qhk/dot_general | solution.py:16
  137.2 50.7 %pmax.7 = f32[512,16]{0,1:T(8,128)S(1)} all-reduce(f32[512,16]{0,1:T(8,128)S(1)} %broadcast_maximum_fusion), channel_id=1, replica_groups=mesh['view'=16,'tok'=16] {'tok'}, use_global_device_ids=true, to_apply=%region_2.3 | all-reduce | flops 8192 | bytes 65536 | tf_op jit(solution)/shard_map/pmax | solution.py:55
  187.8 8.2 %fusion.5 = f32[512,16]{0,1:T(8,128)S(1)} fusion(f32[16,512,512]{2,1,0:T(8,128)} %get-tuple-element.9, f32[512,16]{0,1:T(8,128)S(1)} %broadcast_maximum_fusion, pred[512]{0:T(512)(128)(4,1)S(1)} %broadcast_in_dim.58), kind=kLoop, calls=%fused_computation.10 | loop fusion | flops 20963328 | bytes 16843264 | tf_op jit(solution)/shard_map/reduce_sum | solution.py:22
  196.0 0.8 copy.73
  196.9 6.2 %all-gather.12.cloned.1.call-done = bf16[16,32,1024]{2,1,0:T(8,128)(2,1)} async-done(((bf16[1,32,1024]{2,1,0:T(8,128)(2,1)}), bf16[16,32,1024]{2,1,0:T(8,128)(2,1)}) %all-gather.12.cloned.1.call-update) | async-done | bytes 1048592 | tf_op jit(solution)/shard_map/all_gather | solution.py:41
  203.1 4.1 reshape.121
  207.1 11.6 %bitcast_multiply_fusion = f32[512,16,64]{0,2,1:T(8,128)} fusion(f32[16,512,512]{2,1,0:T(8,128)} %get-tuple-element.9, f32[512,16]{0,1:T(8,128)S(1)} %broadcast_maximum_fusion, pred[512]{0:T(512)(128)(4,1)S(1)} %broadcast_in_dim.58, bf16[512,16,64]{2,1,0:T(8,128)(2,1)} %reshape.121, f32[512,16]{0,1:T(8,128)S(1)} %get-tuple-element.5), kind=kOutput, calls=%fused_computation.21 | convolution fusion | flops 558366720 | bytes 19988992 | tf_op jit(solution)/shard_map/qhk,khd->qhd/dot_general | solution.py:23
  218.8 4.8 copy.60
  223.6 0.2 all-gather.16.cloned.1.call-start
  223.9 42.9 %reduce-scatter.7.cloned.1.call-done = f32[32,16]{1,0:T(8,128)} async-done(((f32[512,16]{1,0:T(8,128)}), f32[32,16]{1,0:T(8,128)}) %reduce-scatter.7.cloned.1.call-update) | async-done | bytes 2064 | tf_op jit(solution)/shard_map/reduce_scatter | solution.py:59
  266.7 70.7 %reduce-scatter.5.cloned.1.call-done = f32[32,16,64]{2,1,0:T(8,128)} async-done(((f32[512,16,64]{2,1,0:T(8,128)}), f32[32,16,64]{2,1,0:T(8,128)}) %reduce-scatter.5.cloned.1.call-update) | async-done | bytes 131088 | tf_op jit(solution)/shard_map/reduce_scatter | solution.py:58
  337.4 1.5 multiply_reduce_fusion.1
  338.9 0.1 reshape.123
  339.1 0.6 multiply_reduce_fusion.2
  339.7 4.0 convolution_convert_fusion
  343.7 1.0 reshape.124
  344.7 1.8 copy.62
  346.5 1.4 reshape.133
  347.9 14.7 %all_to_all.28 = bf16[16,2,3072]{2,1,0:T(2,128)(2,1)} all-to-all(bf16[16,2,3072]{2,1,0:T(2,128)(2,1)} %reshape.133), channel_id=1, replica_groups=mesh['view'=16,'tok'=16] {'tok'}, dimensions={0} | all-to-all | bytes 393216 | tf_op jit(solution)/shard_map/all_to_all | solution.py:75
  362.6 1.6 reshape.134
  364.2 1.3 copy.72
  365.4 1.7 fusion.55
  367.2 0.7 all-gather.14.cloned.1.call-update
  367.9 0.1 reshape.122
  368.0 79.9 %all-gather.16.cloned.1.call-done = bf16[8192,1,64]{2,0,1:T(8,128)(2,1)} async-done(((bf16[512,1,64]{2,0,1:T(8,128)(2,1)}), bf16[8192,1,64]{2,0,1:T(8,128)(2,1)}) %all-gather.16.cloned.1.call-update) | async-done | bytes 1048592 | tf_op jit(solution)/shard_map/all_gather | solution.py:85
  447.9 9.6 %multiply_reduce_fusion = (f32[512]{0:T(512)S(1)}, f32[8192,512]{1,0:T(8,128)}) fusion(bf16[512,3,64]{2,0,1:T(8,128)(2,1)} %bitcast.108, bf16[8192,1,64]{2,0,1:T(8,128)(2,1)} %all-gather.16.cloned.1.call-done), kind=kOutput, calls=%fused_computation.7 | convolution fusion | flops 545259008 | bytes 19007488 | tf_op jit(solution)/shard_map/qhd,khd->qhk/dot_general | solution.py:16
  457.6 8.6 %fusion.3 = f32[512]{0:T(512)S(1)} fusion(f32[8192,512]{1,0:T(8,128)} %get-tuple-element.13, f32[512]{0:T(512)S(1)} %broadcast_maximum_fusion.1), kind=kLoop, calls=%fused_computation.8 | loop fusion | flops 12582400 | bytes 16781312 | tf_op jit(solution)/shard_map/reduce_sum | solution.py:22
  466.2 67.0 %all-gather.14.cloned.1.call-done = bf16[8192,1,64]{2,0,1:T(8,128)(2,1)} async-done(((bf16[512,1,64]{2,0,1:T(8,128)(2,1)}), bf16[8192,1,64]{2,0,1:T(8,128)(2,1)}) %all-gather.14.cloned.1.call-update) | async-done | bytes 1048592 | tf_op jit(solution)/shard_map/all_gather | solution.py:86
  533.2 9.3 %fusion.39 = bf16[512,1,64]{0,2,1:T(8,128)(2,1)S(1)} fusion(f32[8192,512]{1,0:T(8,128)} %get-tuple-element.13, f32[512]{0:T(512)S(1)} %broadcast_maximum_fusion.1, bf16[8192,1,64]{2,0,1:T(8,128)(2,1)} %all-gather.14.cloned.1.call-done, f32[512]{0:T(512)S(1)} %fusion.3), kind=kOutput, calls=%fused_computation.30 | convolution fusion | flops 549519360 | bytes 17895424 | tf_op jit(solution)/shard_map/qhk,khd->qhd/dot_general | solution.py:23
  542.5 0.1 copy.68
  542.7 0.8 reshape.135
  543.4 8.6 %all-to-all-start.1 = ((bf16[16,2,1024]{2,1,0:T(2,128)(2,1)}), bf16[16,2,1024]{2,1,0:T(2,128)(2,1)S(1)}, u32[]{:S(2)}, u32[]{:S(2)}) async-start(bf16[16,2,1024]{2,1,0:T(2,128)(2,1)} %reshape.135), calls=%async_computation.2 | async-start | bytes 131072 | tf_op jit(solution)/shard_map/all_to_all | solution.py:97
  552.0 0.7 broadcast_multiply_fusion
  552.8 5.1 all-to-all-done.1
  557.8 0.1 reshape.136
  558.0 0.1 fusion.44
  558.2 0.2 copy.69
  558.3 0.1 reshape.128
  558.5 2.8 convolution_bitcast_fusion
  (24 shorter events, 0.5 us)
Async XLA Ops:
  7.2 331.9 %copy-start = (bf16[1024,1024]{1,0:T(8,128)(2,1)S(1)}, bf16[1024,1024]{1,0:T(8,128)(2,1)}, u32[]{:S(2)}) copy-start(bf16[1024,1024]{1,0:T(8,128)(2,1)} %param.14) | copy-start | bytes 6291460
  7.2 81.6 %all-gather.8.cloned.1.call-start = ((), (), s32[]{:S(2)}) async-start(), calls=%async_computation.4 | async-start | bytes 1114112 | tf_op jit(solution)/shard_map/all_gather | solution.py:40
  7.9 118.7 %all-gather.10.cloned.1.call-start = ((), (), s32[]{:S(2)}) async-start(), calls=%async_computation.5 | async-start | bytes 1114112 | tf_op jit(solution)/shard_map/all_gather | solution.py:32
  8.7 194.4 %all-gather.12.cloned.1.call-start = ((), (), s32[]{:S(2)}) async-start(), calls=%async_computation.6 | async-start | bytes 1114112 | tf_op jit(solution)/shard_map/all_gather | solution.py:41
  9.4 257.3 %reduce-scatter.7.cloned.1.call-start = ((), (), s32[]{:S(2)}) async-start(), calls=%async_computation.10 | async-start | bytes 278528 | tf_op jit(solution)/shard_map/reduce_scatter | solution.py:59
  196.9 140.5 %reduce-scatter.5.cloned.1.call-start = ((), (), s32[]{:S(2)}) async-start(), calls=%async_computation.7 | async-start | bytes 4456448 | tf_op jit(solution)/shard_map/reduce_scatter | solution.py:58
  207.1 131.9 %copy-start.1 = (bf16[1,32,1024]{2,1,0:T(8,128)(2,1)S(1)}, bf16[1,32,1024]{2,1,0:T(8,128)(2,1)}, u32[]{:S(2)}) copy-start(bf16[1,32,1024]{2,1,0:T(8,128)(2,1)} %param.13) | copy-start | bytes 196612
  207.1 132.6 %copy-start.2 = (f32[1024]{0:T(1024)S(1)}, f32[1024]{0:T(1024)}, u32[]{:S(2)}) copy-start(f32[1024]{0:T(1024)} %param.15) | copy-start | bytes 12292
  223.6 224.3 %all-gather.16.cloned.1.call-start = ((), (), s32[]{:S(2)}) async-start(), calls=%async_computation.9 | async-start | bytes 2228224 | tf_op jit(solution)/shard_map/all_gather | solution.py:85
  367.1 166.1 %all-gather.14.cloned.1.call-start = ((), (), s32[]{:S(2)}) async-start(), calls=%async_computation.8 | async-start | bytes 2228224 | tf_op jit(solution)/shard_map/all_gather | solution.py:86
  543.4 14.4 %all-to-all-start.1 = ((bf16[16,2,1024]{2,1,0:T(2,128)(2,1)}), bf16[16,2,1024]{2,1,0:T(2,128)(2,1)S(1)}, u32[]{:S(2)}, u32[]{:S(2)}) async-start(bf16[16,2,1024]{2,1,0:T(2,128)(2,1)} %reshape.135), calls=%async_computation.2 | async-start | bytes 131072 | tf_op jit(solution)/shard_map/all_to_all | solution.py:97
Sparse Core Ops, SparseCore 0:
  10.6 78.1 all-gather.7
  90.6 35.9 all-gather.9
  129.2 73.8 all-gather.11
  205.4 61.2 reduce-scatter.6
  269.1 68.2 reduce-scatter.4
  367.3 80.6 all-gather.15
  451.1 82.0 all-gather.13
where the time goes:
time: 569 us; the launch traced here: 568 us
  waiting for transfers between devices  387 us (68%)
  blocking collectives  65.4 us (11%)
  matrix products  47.1 us (8%)
  local copies, waits for them, and re-layouts  25.7 us (5%)
  other arithmetic  20 us (4%)
  between operations  14.3 us (3%)
  starting transfers between devices  9.04 us (2%)
    all_gather x1, waiting for transfers between devices, per_device(): key_piece = lax.all_gather(by_head[:, 1], 'view', axis=0, tiled=True)  79.9 us
    all_gather x1, waiting for transfers between devices, per_device(): key_piece = lax.all_gather(k1, 'view', axis=0, tiled=True)  78.4 us
    reduce_scatter x1, waiting for transfers between devices, per_device(): lax.psum_scatter(weighted * factor[..., None], 'tok', scatter_dimension=0...  70.7 us
    all_gather x1, waiting for transfers between devices, per_device(): val_piece = lax.all_gather(by_head[:, 2], 'view', axis=0, tiled=True)  67 us
    pmax x1, blocking collectives, per_device(): row_peak = lax.pmax(running_max, 'tok')  50.7 us
    reduce_scatter x1, waiting for transfers between devices, per_device(): lax.psum_scatter(row_total * factor, 'tok', scatter_dimension=0, tiled=True)  42.9 us
    all_gather x1, waiting for transfers between devices, per_device(): lax.all_gather(q1, 'tok', axis=1, tiled=True)[0].reshape(-1, H1, HD1)  33.8 us
    dot_general x2, matrix products, absorb(): jnp.einsum('qhk,khd->qhd', weights.astype(jnp.bfloat16), val_piece, prefe...  21 us
  transfers between devices with their start and end apart: 8, of which 8 were waited for; matrix products, arithmetic and copies ran while one was open for 11% of the time, Pallas kernels for 0%

commit v1 on v0

--- a/solution.py
+++ b/solution.py
@@ -37,7 +37,9 @@
         jnp.zeros((query_rows, H1, HD1), jnp.float32),
     )
     scale_one = HD1 ** (-0.5)
-    key_piece = lax.all_gather(k1, "view", axis=0, tiled=True)
+    key_piece = jnp.concatenate(
+        lax.all_to_all(jnp.stack([k1] * lax.axis_size("view")), "view", 0, 0), axis=0
+    )
     val_piece = lax.all_gather(v1, "view", axis=0, tiled=True)
     view_ids = jnp.arange(key_piece.shape[0], dtype=jnp.int32)
     keep_view = (view_ids == own_view) | jnp.any(view_ids[:, None] == wanted[None, :], axis=1)

time: 569 us -> 498 us (0.88)
  waiting for transfers between devices: 387 us -> 301 us
  starting transfers between devices: 9.04 us -> 20.7 us
    all_gather x1 -> x0, waiting for transfers between devices: 78.4 us -> none  [per_device(): key_piece = lax.all_gather(k1, 'view', axis=0, tiled=True)]
    all_gather x1, waiting for transfers between devices: 33.8 us -> 0.01 us  [per_device(): lax.all_gather(q1, 'tok', axis=1, tiled=True)[0].reshape(-1, H1, HD1)]
    all_to_all x0 -> x1, waiting for transfers between devices: none -> 25.2 us  [per_device(): lax.all_to_all(jnp.stack([k1] * lax.axis_size('view')), 'view', 0, 0)]
    all_to_all x0 -> x1, starting transfers between devices: none -> 11.7 us  [per_device(): lax.all_to_all(jnp.stack([k1] * lax.axis_size('view')), 'view', 0, 0)]
  transfers between devices with their start and end apart: 8 -> 8, of which waited for: 8 -> 7; matrix products, arithmetic and copies ran while one was open for 11% -> 13% of each run, Pallas kernels for 0% -> 0%
where the time goes in v1:
time: 498 us; the launch traced here: 497 us
  waiting for transfers between devices  301 us (60%)
  blocking collectives  67.6 us (14%)
  matrix products  47.1 us (9%)
  local copies, waits for them, and re-layouts  26 us (5%)
  starting transfers between devices  20.7 us (4%)
  other arithmetic  20 us (4%)
  between operations  14.3 us (3%)
    all_gather x1, waiting for transfers between devices, per_device(): key_piece = lax.all_gather(by_head[:, 1], 'view', axis=0, tiled=True)  80.1 us
    reduce_scatter x1, waiting for transfers between devices, per_device(): lax.psum_scatter(weighted * factor[..., None], 'tok', scatter_dimension=0...  70.8 us
    all_gather x1, waiting for transfers between devices, per_device(): val_piece = lax.all_gather(by_head[:, 2], 'view', axis=0, tiled=True)  66.9 us
    pmax x1, blocking collectives, per_device(): row_peak = lax.pmax(running_max, 'tok')  52.9 us
    reduce_scatter x1, waiting for transfers between devices, per_device(): lax.psum_scatter(row_total * factor, 'tok', scatter_dimension=0, tiled=True)  42.9 us
    all_to_all x1, waiting for transfers between devices, per_device(): lax.all_to_all(jnp.stack([k1] * lax.axis_size('view')), 'view', 0, 0)  25.2 us
    dot_general x2, matrix products, absorb(): jnp.einsum('qhk,khd->qhd', weights.astype(jnp.bfloat16), val_piece, prefe...  21 us
    dot_general x2, matrix products, absorb(): jnp.einsum('qhd,khd->qhk', queries, key_piece, preferred_element_type=jnp...  18.7 us
  transfers between devices with their start and end apart: 8, of which 7 were waited for; matrix products, arithmetic and copies ran while one was open for 13% of the time, Pallas kernels for 0%

profile of v1, /device:TPU:1, one launch (start us, length us, event | category | flops | bytes accessed | tf_op | source)
XLA Modules:
  0.0 497.0 jit_solution(14444554555558259861)
XLA Ops:
  7.2 0.7 all-gather.7.cloned.1.call-update
  7.9 2.0 stack.2
  9.9 11.7 %all-to-all-start = ((bf16[16,1,32,1024]{3,2,1,0:T(8,128)(2,1)}), bf16[16,1,32,1024]{3,2,1,0:T(8,128)(2,1)S(1)}, u32[]{:S(2)}, u32[]{:S(2)}) async-start(bf16[16,1,32,1024]{3,2,1,0:T(8,128)(2,1)} %stack.2), calls=%async_computation | async-start | bytes 2097152 | tf_op jit(solution)/shard_map/all_to_all | solution.py:41
  21.7 0.7 all-gather.9.cloned.1.call-update
  22.5 0.7 fusion.49
  23.3 0.1 broadcast_in_dim.58
  23.4 25.2 %all-to-all-done = bf16[16,1,32,1024]{3,2,1,0:T(8,128)(2,1)S(1)} async-done(((bf16[16,1,32,1024]{3,2,1,0:T(8,128)(2,1)}), bf16[16,1,32,1024]{3,2,1,0:T(8,128)(2,1)S(1)}, u32[]{:S(2)}, u32[]{:S(2)}) %all-to-all-start) | async-done | bytes 1048608 | tf_op jit(solution)/shard_map/all_to_all | solution.py:41
  48.6 2.4 reshape_reshape.3
  50.9 1.5 copy.56
  52.4 9.1 %bitcast_reduce_fusion = (f32[512,16]{0,1:T(8,128)S(1)}, f32[16,512,512]{2,1,0:T(8,128)}) fusion(pred[512]{0:T(512)(128)(4,1)S(1)} %broadcast_in_dim.58, bf16[512,16,64]{0,2,1:T(8,128)(2,1)S(1)} %bitcast.107, bf16[512,16,64]{2,1,0:T(8,128)(2,1)} %reshape_reshape.3), kind=kOutput, calls=%fused_computation.3 | convolution fusion | flops 549445632 | bytes 18907648 | tf_op jit(solution)/shard_map/qhd,khd->qhk/dot_general | solution.py:16
  61.5 52.9 %pmax.7 = f32[512,16]{0,1:T(8,128)S(1)} all-reduce(f32[512,16]{0,1:T(8,128)S(1)} %broadcast_maximum_fusion), channel_id=1, replica_groups=mesh['view'=16,'tok'=16] {'tok'}, use_global_device_ids=true, to_apply=%region_2.3 | all-reduce | flops 8192 | bytes 65536 | tf_op jit(solution)/shard_map/pmax | solution.py:57
  114.4 8.1 %fusion.5 = f32[512,16]{0,1:T(8,128)S(1)} fusion(f32[16,512,512]{2,1,0:T(8,128)} %get-tuple-element.9, f32[512,16]{0,1:T(8,128)S(1)} %broadcast_maximum_fusion, pred[512]{0:T(512)(128)(4,1)S(1)} %broadcast_in_dim.58), kind=kLoop, calls=%fused_computation.10 | loop fusion | flops 20963328 | bytes 16843264 | tf_op jit(solution)/shard_map/reduce_sum | solution.py:22
  122.6 0.8 copy.73
  123.5 8.5 %all-gather.9.cloned.1.call-done = bf16[16,32,1024]{2,1,0:T(8,128)(2,1)} async-done(((bf16[1,32,1024]{2,1,0:T(8,128)(2,1)}), bf16[16,32,1024]{2,1,0:T(8,128)(2,1)}) %all-gather.9.cloned.1.call-update) | async-done | bytes 1048592 | tf_op jit(solution)/shard_map/all_gather | solution.py:43
  132.0 4.1 reshape.120
  136.1 11.6 %bitcast_multiply_fusion = f32[512,16,64]{0,2,1:T(8,128)} fusion(f32[16,512,512]{2,1,0:T(8,128)} %get-tuple-element.9, f32[512,16]{0,1:T(8,128)S(1)} %broadcast_maximum_fusion, pred[512]{0:T(512)(128)(4,1)S(1)} %broadcast_in_dim.58, bf16[512,16,64]{2,1,0:T(8,128)(2,1)} %reshape.120, f32[512,16]{0,1:T(8,128)S(1)} %get-tuple-element.5), kind=kOutput, calls=%fused_computation.21 | convolution fusion | flops 558366720 | bytes 19988992 | tf_op jit(solution)/shard_map/qhk,khd->qhd/dot_general | solution.py:23
  147.7 4.8 copy.60
  152.6 0.2 all-gather.13.cloned.1.call-start
  152.8 42.9 %reduce-scatter.7.cloned.1.call-done = f32[32,16]{1,0:T(8,128)} async-done(((f32[512,16]{1,0:T(8,128)}), f32[32,16]{1,0:T(8,128)}) %reduce-scatter.7.cloned.1.call-update) | async-done | bytes 2064 | tf_op jit(solution)/shard_map/reduce_scatter | solution.py:61
  195.7 70.8 %reduce-scatter.5.cloned.1.call-done = f32[32,16,64]{2,1,0:T(8,128)} async-done(((f32[512,16,64]{2,1,0:T(8,128)}), f32[32,16,64]{2,1,0:T(8,128)}) %reduce-scatter.5.cloned.1.call-update) | async-done | bytes 131088 | tf_op jit(solution)/shard_map/reduce_scatter | solution.py:60
  266.5 1.5 multiply_reduce_fusion.1
  268.0 0.1 reshape.122
  268.2 0.6 multiply_reduce_fusion.2
  268.8 4.0 convolution_convert_fusion
  272.8 1.0 reshape.123
  273.8 1.8 copy.62
  275.6 1.4 reshape.132
  277.0 14.7 %all_to_all.33 = bf16[16,2,3072]{2,1,0:T(2,128)(2,1)} all-to-all(bf16[16,2,3072]{2,1,0:T(2,128)(2,1)} %reshape.132), channel_id=1, replica_groups=mesh['view'=16,'tok'=16] {'tok'}, dimensions={0} | all-to-all | bytes 393216 | tf_op jit(solution)/shard_map/all_to_all | solution.py:77
  291.7 1.6 reshape.133
  293.3 1.3 copy.72
  294.5 1.7 fusion.55
  296.3 0.5 all-gather.11.cloned.1.call-update
  296.8 0.1 reshape.121
  297.0 80.1 %all-gather.13.cloned.1.call-done = bf16[8192,1,64]{2,0,1:T(8,128)(2,1)} async-done(((bf16[512,1,64]{2,0,1:T(8,128)(2,1)}), bf16[8192,1,64]{2,0,1:T(8,128)(2,1)}) %all-gather.13.cloned.1.call-update) | async-done | bytes 1048592 | tf_op jit(solution)/shard_map/all_gather | solution.py:87
  377.1 9.6 %multiply_reduce_fusion = (f32[512]{0:T(512)S(1)}, f32[8192,512]{1,0:T(8,128)}) fusion(bf16[512,3,64]{2,0,1:T(8,128)(2,1)} %bitcast.111, bf16[8192,1,64]{2,0,1:T(8,128)(2,1)} %all-gather.13.cloned.1.call-done), kind=kOutput, calls=%fused_computation.7 | convolution fusion | flops 545259008 | bytes 19007488 | tf_op jit(solution)/shard_map/qhd,khd->qhk/dot_general | solution.py:16
  386.7 8.6 %fusion.3 = f32[512]{0:T(512)S(1)} fusion(f32[8192,512]{1,0:T(8,128)} %get-tuple-element.13, f32[512]{0:T(512)S(1)} %broadcast_maximum_fusion.1), kind=kLoop, calls=%fused_computation.8 | loop fusion | flops 12582400 | bytes 16781312 | tf_op jit(solution)/shard_map/reduce_sum | solution.py:22
  395.3 66.9 %all-gather.11.cloned.1.call-done = bf16[8192,1,64]{2,0,1:T(8,128)(2,1)} async-done(((bf16[512,1,64]{2,0,1:T(8,128)(2,1)}), bf16[8192,1,64]{2,0,1:T(8,128)(2,1)}) %all-gather.11.cloned.1.call-update) | async-done | bytes 1048592 | tf_op jit(solution)/shard_map/all_gather | solution.py:88
  462.2 9.3 %fusion.39 = bf16[512,1,64]{0,2,1:T(8,128)(2,1)S(1)} fusion(f32[8192,512]{1,0:T(8,128)} %get-tuple-element.13, f32[512]{0:T(512)S(1)} %broadcast_maximum_fusion.1, bf16[8192,1,64]{2,0,1:T(8,128)(2,1)} %all-gather.11.cloned.1.call-done, f32[512]{0:T(512)S(1)} %fusion.3), kind=kOutput, calls=%fused_computation.30 | convolution fusion | flops 549519360 | bytes 17895424 | tf_op jit(solution)/shard_map/qhk,khd->qhd/dot_general | solution.py:23
  471.5 0.1 copy.68
  471.6 0.8 reshape.134
  472.4 8.6 %all-to-all-start.2 = ((bf16[16,2,1024]{2,1,0:T(2,128)(2,1)}), bf16[16,2,1024]{2,1,0:T(2,128)(2,1)S(1)}, u32[]{:S(2)}, u32[]{:S(2)}) async-start(bf16[16,2,1024]{2,1,0:T(2,128)(2,1)} %reshape.134), calls=%async_computation.3 | async-start | bytes 131072 | tf_op jit(solution)/shard_map/all_to_all | solution.py:99
  481.0 0.7 broadcast_multiply_fusion
  481.7 5.1 %all-to-all-done.2 = bf16[16,2,1024]{2,1,0:T(2,128)(2,1)S(1)} async-done(((bf16[16,2,1024]{2,1,0:T(2,128)(2,1)}), bf16[16,2,1024]{2,1,0:T(2,128)(2,1)S(1)}, u32[]{:S(2)}, u32[]{:S(2)}) %all-to-all-start.2) | async-done | bytes 65568 | tf_op jit(solution)/shard_map/all_to_all | solution.py:99
  486.8 0.1 reshape.135
  487.0 0.1 fusion.44
  487.1 0.2 copy.69
  487.3 0.1 reshape.127
  487.4 2.8 convolution_bitcast_fusion
  (24 shorter events, 0.4 us)
Async XLA Ops:
  7.2 261.0 %copy-start = (bf16[1024,1024]{1,0:T(8,128)(2,1)S(1)}, bf16[1024,1024]{1,0:T(8,128)(2,1)}, u32[]{:S(2)}) copy-start(bf16[1024,1024]{1,0:T(8,128)(2,1)} %param.14) | copy-start | bytes 6291460
  7.2 43.8 %all-gather.7.cloned.1.call-start = ((), (), s32[]{:S(2)}) async-start(), calls=%async_computation.5 | async-start | bytes 1114112 | tf_op jit(solution)/shard_map/all_gather | solution.py:32
  9.9 38.7 %all-to-all-start = ((bf16[16,1,32,1024]{3,2,1,0:T(8,128)(2,1)}), bf16[16,1,32,1024]{3,2,1,0:T(8,128)(2,1)S(1)}, u32[]{:S(2)}, u32[]{:S(2)}) async-start(bf16[16,1,32,1024]{3,2,1,0:T(8,128)(2,1)} %stack.2), calls=%async_computation | async-start | bytes 2097152 | tf_op jit(solution)/shard_map/all_to_all | solution.py:41
  21.7 110.4 %all-gather.9.cloned.1.call-start = ((), (), s32[]{:S(2)}) async-start(), calls=%async_computation.6 | async-start | bytes 1114112 | tf_op jit(solution)/shard_map/all_gather | solution.py:43
  22.4 173.3 %reduce-scatter.7.cloned.1.call-start = ((), (), s32[]{:S(2)}) async-start(), calls=%async_computation.10 | async-start | bytes 278528 | tf_op jit(solution)/shard_map/reduce_scatter | solution.py:61
  123.5 143.0 %reduce-scatter.5.cloned.1.call-start = ((), (), s32[]{:S(2)}) async-start(), calls=%async_computation.7 | async-start | bytes 4456448 | tf_op jit(solution)/shard_map/reduce_scatter | solution.py:60
  136.1 132.1 %copy-start.1 = (bf16[1,32,1024]{2,1,0:T(8,128)(2,1)S(1)}, bf16[1,32,1024]{2,1,0:T(8,128)(2,1)}, u32[]{:S(2)}) copy-start(bf16[1,32,1024]{2,1,0:T(8,128)(2,1)} %param.13) | copy-start | bytes 196612
  136.1 132.7 %copy-start.2 = (f32[1024]{0:T(1024)S(1)}, f32[1024]{0:T(1024)}, u32[]{:S(2)}) copy-start(f32[1024]{0:T(1024)} %param.15) | copy-start | bytes 12292
  152.6 224.5 %all-gather.13.cloned.1.call-start = ((), (), s32[]{:S(2)}) async-start(), calls=%async_computation.9 | async-start | bytes 2228224 | tf_op jit(solution)/shard_map/all_gather | solution.py:87
  296.3 165.9 %all-gather.11.cloned.1.call-start = ((), (), s32[]{:S(2)}) async-start(), calls=%async_computation.8 | async-start | bytes 2228224 | tf_op jit(solution)/shard_map/all_gather | solution.py:88
  472.4 14.4 %all-to-all-start.2 = ((bf16[16,2,1024]{2,1,0:T(2,128)(2,1)}), bf16[16,2,1024]{2,1,0:T(2,128)(2,1)S(1)}, u32[]{:S(2)}, u32[]{:S(2)}) async-start(bf16[16,2,1024]{2,1,0:T(2,128)(2,1)} %reshape.134), calls=%async_computation.3 | async-start | bytes 131072 | tf_op jit(solution)/shard_map/all_to_all | solution.py:99
Sparse Core Ops, SparseCore 0:
  9.8 40.9 all-gather.6
  53.4 78.5 all-gather.8
  134.5 61.1 reduce-scatter.6
  198.1 68.3 reduce-scatter.4
  296.4 80.6 all-gather.12
  380.1 82.0 all-gather.10
